TPU v7x, 512 devices: a whole 4x4x16 slice. The times are simulated.
512 devices in a mesh: len: 128 (over y, z, core), pipe: 4 (over x).
Axes of the slice: x: 4, y: 4, z: 16, core: 2. Of those that a mesh axis runs over, the one named last changes fastest.
Arguments:
- inputs: bfloat16 [512, 2048, 256], P(('len', 'pipe')), may hold values from -6 to 6
- cotangent: bfloat16 [512, 2048, 256], P(('len', 'pipe')), may hold values from -6 to 6
- point_weight: bfloat16 [256, 256], replicated, may hold values from -0.375 to 0.375
- point_bias: float32 [256], replicated, may hold values from -3 to 3
- spec_real: bfloat16 [128, 256, 256], P('len'), may hold values from -0.25 to 0.25
- spec_imag: bfloat16 [128, 256, 256], P('len'), may hold values from -0.25 to 0.25
- junc_weight: bfloat16 [256, 256], replicated, may hold values from -0.375 to 0.375
- junc_bias: float32 [256], replicated, may hold values from -3 to 3
- inlet_ids: int32 [512], replicated, may hold values from 0 to 511
- outlet_ids: int32 [512], replicated, may hold values from 0 to 511
Outputs:
- outputs: bfloat16 [512, 2048, 256], P(('len', 'pipe'))
- grad_inputs: bfloat16 [512, 2048, 256], P(('len', 'pipe'))
- grad_real: float32 [128, 256, 256], P('len')
- grad_imag: float32 [128, 256, 256], P('len')
All inputs are finite; a program needn't handle non-finite values.
Results may differ from a plain program's by a relative error of at most 0.015.
Values may be sent and summed in bfloat16 or wider, within the bound.
A program may use at most 64 MiB of HBM per device.

v0:
```python
import math
import jax
import jax.numpy as jnp
from jax import lax
from jax.sharding import PartitionSpec as P

COUPLING = 0.125


def tables(cell_count, mode_count):
    position = lax.broadcasted_iota(jnp.int32, (mode_count, cell_count), 1)
    frequency = lax.broadcasted_iota(jnp.int32, (mode_count, cell_count), 0)
    product_index = frequency * position % cell_count
    angles = product_index.astype(jnp.float32) * (2.0 * math.pi / cell_count)
    norm_scale = 1.0 / math.sqrt(cell_count)
    cosine = jnp.cos(angles) * norm_scale
    sine_table = jnp.sin(angles) * norm_scale
    doubled = jnp.where(frequency == 0, 1.0, 2.0)
    forward = (
        jnp.stack([cosine, -sine_table], axis=1)
        .reshape(2 * mode_count, cell_count)
        .astype(jnp.bfloat16)
    )
    inverse = jnp.transpose(
        jnp.stack([doubled * cosine, -doubled * sine_table], axis=1).reshape(
            2 * mode_count, cell_count
        )
    ).astype(jnp.bfloat16)
    return (forward, inverse)


def spectral_blocks(spec_real, spec_imag):
    upper = jnp.concatenate([spec_real, spec_imag], axis=2)
    lower = jnp.concatenate([-spec_imag, spec_real], axis=2)
    return jnp.concatenate([upper, lower], axis=1)


def activate(values):
    return jax.nn.gelu(values, approximate=True)


def silu_slope(values):
    sigmoid_part = jax.nn.sigmoid(values)
    return sigmoid_part * (1.0 + values * (1.0 - sigmoid_part))


def to_modes(field):
    return lax.all_to_all(field, "len", split_axis=1, concat_axis=0, tiled=True)


def from_modes(field):
    return lax.all_to_all(field, "len", split_axis=0, concat_axis=1, tiled=True)


def body(
    inputs,
    cotangent,
    point_weight,
    point_bias,
    spec_real,
    spec_imag,
    junc_weight,
    junc_bias,
    inlet_ids,
    outlet_ids,
):
    per_dev, cell_count, channels = inputs.shape
    len_count = lax.axis_size("len")
    mode_count = spec_real.shape[0] * len_count
    junc_count = inlet_ids.shape[0]
    forward, inverse = tables(cell_count, mode_count)
    blocks = spectral_blocks(spec_real, spec_imag)
    start = (lax.axis_index("len") * lax.axis_size("pipe") + lax.axis_index("pipe")) * per_dev
    my_inlets = lax.dynamic_slice_in_dim(inlet_ids, start, per_dev)
    my_outlets = lax.dynamic_slice_in_dim(outlet_ids, start, per_dev)
    mine = jnp.concatenate([my_inlets, my_outlets])[:, None]
    in_match = mine == inlet_ids[None, :]
    out_match = mine == outlet_ids[None, :]
    end_rows = lax.all_gather(
        jnp.stack([inputs[:, 0, :], inputs[:, -1, :]]), ("len", "pipe"), axis=1, tiled=True
    )
    spectra = jnp.einsum("kl,plc->pkc", forward, inputs, preferred_element_type=jnp.float32).astype(
        jnp.bfloat16
    )
    mode_rows = to_modes(spectra.reshape(per_dev, mode_count, 2, channels))
    mode_rows = mode_rows.reshape(mode_rows.shape[0], -1, 2 * channels)
    mixed = jnp.einsum(
        "pmk,mkn->pmn", mode_rows, blocks, preferred_element_type=jnp.float32
    ).astype(jnp.bfloat16)
    returned_modes = from_modes(mixed.reshape(mixed.shape[0], -1, 2, channels)).reshape(
        per_dev, 2 * mode_count, channels
    )
    junc_sums = jnp.dot(
        in_match.astype(jnp.bfloat16), end_rows[0], preferred_element_type=jnp.float32
    ) + jnp.dot(out_match.astype(jnp.bfloat16), end_rows[1], preferred_element_type=jnp.float32)
    junc_act = (
        jnp.dot(junc_sums.astype(jnp.bfloat16), junc_weight, preferred_element_type=jnp.float32)
        + junc_bias
    )
    junc_rows = jax.nn.silu(junc_act).astype(jnp.bfloat16).astype(jnp.float32)
    cond = COUPLING * (junc_rows[:per_dev] + junc_rows[per_dev:])
    spectral = jnp.einsum(
        "lk,pkc->plc", inverse, returned_modes, preferred_element_type=jnp.float32
    )
    pre = (spectral + cond[:, None, :]).astype(jnp.bfloat16)
    pointwise = jnp.dot(
        inputs.reshape(-1, channels), point_weight, preferred_element_type=jnp.float32
    ).reshape(inputs.shape)
    summed = pointwise + point_bias + pre.astype(jnp.float32)
    result, pullback = jax.vjp(activate, summed)
    outputs = result.astype(jnp.bfloat16)
    grad_total = pullback(cotangent.astype(jnp.float32))[0].astype(jnp.bfloat16)
    grad_spec = jnp.einsum(
        "lk,plc->pkc", inverse, grad_total, preferred_element_type=jnp.float32
    ).astype(jnp.bfloat16)
    grad_modes = to_modes(grad_spec.reshape(per_dev, mode_count, 2, channels))
    grad_modes = grad_modes.reshape(grad_modes.shape[0], -1, 2 * channels)
    grad_mixed = jnp.einsum(
        "pmn,mkn->pmk", grad_modes, blocks, preferred_element_type=jnp.float32
    ).astype(jnp.bfloat16)
    weight_terms = jnp.einsum(
        "pmk,pmn->mkn", mode_rows, grad_modes, preferred_element_type=jnp.float32
    )
    real_terms = weight_terms[:, :channels, :channels] + weight_terms[:, channels:, channels:]
    imag_terms = weight_terms[:, :channels, channels:] - weight_terms[:, channels:, :channels]
    grad_real, grad_imag = (
        jnp.sum(
            lax.all_gather(real_terms.astype(jnp.bfloat16), "pipe").astype(jnp.float32), axis=0
        ),
        jnp.sum(
            lax.all_gather(imag_terms.astype(jnp.bfloat16), "pipe").astype(jnp.float32), axis=0
        ),
    )
    grad_back = from_modes(grad_mixed.reshape(grad_mixed.shape[0], -1, 2, channels)).reshape(
        per_dev, 2 * mode_count, channels
    )
    grad_cells = jnp.einsum("kl,pkc->plc", forward, grad_back, preferred_element_type=jnp.float32)
    grad_cond = jnp.sum(grad_total, axis=1, dtype=jnp.float32)
    all_cond = lax.all_gather(grad_cond, ("len", "pipe"), axis=0, tiled=True)
    junc_grad = COUPLING * jnp.dot(
        in_match.astype(jnp.float32) + out_match.astype(jnp.float32),
        all_cond,
        precision=lax.Precision.HIGHEST,
    )
    act_grad = (junc_grad * silu_slope(junc_act)).astype(jnp.bfloat16)
    sums_grad = jnp.dot(act_grad, junc_weight.T, preferred_element_type=jnp.float32).astype(
        jnp.bfloat16
    )
    end_first = sums_grad[:per_dev].astype(jnp.float32)
    end_last = sums_grad[per_dev:].astype(jnp.float32)
    grad_cells = grad_cells.at[:, 0, :].add(end_first).at[:, -1, :].add(end_last)
    spread = grad_cells.astype(jnp.bfloat16)
    grad_local = jnp.dot(
        grad_total.reshape(-1, channels), point_weight.T, preferred_element_type=jnp.float32
    ).reshape(inputs.shape)
    grad_inputs = (grad_local + spread.astype(jnp.float32)).astype(jnp.bfloat16)
    return (outputs, grad_inputs, grad_real, grad_imag)


def solution(mesh):
    placed = (
        P(("len", "pipe"), None, None),
        P(("len", "pipe"), None, None),
        P(),
        P(),
        P("len", None, None),
        P("len", None, None),
        P(),
        P(),
        P(),
        P(),
    )
    return jax.shard_map(
        body,
        mesh=mesh,
        in_specs=placed,
        out_specs=(
            P(("len", "pipe"), None, None),
            P(("len", "pipe"), None, None),
            P("len", None, None),
            P("len", None, None),
        ),
        check_vma=False,
    )
```

profile of v0, /device:TPU:16, one launch (start us, length us, event | category | flops | bytes accessed | tf_op | source)
XLA Modules:
  0.0 529.5 jit_solution(12464476966603268177)
XLA Ops:
  0.6 4.3 negate_convert_fusion
  5.1 1.1 copy.48
  7.1 0.7 reshape.318
  7.8 19.7 %all-to-all-start = ((bf16[1,128,2,256]{3,2,0,1:T(2,128)(2,1)}), bf16[1,128,2,256]{3,2,0,1:T(2,128)(2,1)S(1)}, u32[]{:S(2)}, u32[]{:S(2)}) async-start(bf16[1,128,2,256]{3,2,0,1:T(2,128)(2,1)} %bitcast.6), calls=%async_computation | async-start | bytes 262144 | tf_op jit(solution)/shard_map/all_to_all | solution.py:48
  28.8 1.4 pad_add_fusion
  30.2 4.4 multiply_convert_fusion.1
  34.7 195.5 %all_gather.18 = bf16[2,512,256]{2,0,1:T(2,128)(2,1)S(1)} all-gather(bf16[2,1,256]{2,0,1:T(2,128)(2,1)S(1)} %pad_maximum_fusion.2), channel_id=1, replica_groups=mesh['len'=128,'pipe'=4] {'len','pipe'}, dimensions={1}, use_global_device_ids=true | all-gather | bytes 525312 | tf_op jit(solution)/shard_map/all_gather | solution.py:79
  230.3 1.5 fusion.64
  232.2 0.8 copy.50
  233.0 16.1 %all-to-all-start.1 = ((bf16[128,1,2,256]{3,2,1,0:T(2,128)(2,1)}), bf16[128,1,2,256]{3,2,1,0:T(2,128)(2,1)}, u32[]{:S(2)}, u32[]{:S(2)}) async-start(bf16[128,1,2,256]{3,2,1,0:T(2,128)(2,1)} %copy.50), calls=%async_computation.1 | async-start | bytes 262144 | tf_op jit(solution)/shard_map/all_to_all | solution.py:52
  249.1 0.8 fusion.39
  249.8 1.1 copy.51
  251.4 1.5 fusion.54
  252.9 12.6 %all-to-all-done.1 = bf16[128,1,2,256]{3,2,1,0:T(2,128)(2,1)} async-done(((bf16[128,1,2,256]{3,2,1,0:T(2,128)(2,1)}), bf16[128,1,2,256]{3,2,1,0:T(2,128)(2,1)}, u32[]{:S(2)}, u32[]{:S(2)}) %all-to-all-start.1) | async-done | bytes 131104 | tf_op jit(solution)/shard_map/all_to_all | solution.py:52
  265.5 1.0 reshape.321
  267.0 0.6 copy-done.14
  267.7 3.7 convert_reduce_fusion
  271.4 1.0 copy-done.1
  272.8 0.7 reshape.324
  273.5 7.5 %all-to-all-start.2 = ((bf16[1,128,2,256]{3,2,0,1:T(2,128)(2,1)}), bf16[1,128,2,256]{3,2,0,1:T(2,128)(2,1)S(1)}, u32[]{:S(2)}, u32[]{:S(2)}) async-start(bf16[1,128,2,256]{3,2,0,1:T(2,128)(2,1)} %bitcast.19), calls=%async_computation.2 | async-start | bytes 262144 | tf_op jit(solution)/shard_map/all_to_all | solution.py:48
  281.0 194.3 %all-gather.3 = f32[512,1,256]{2,1,0:T(1,128)S(1)} all-gather(f32[1,1,256]{2,1,0:T(1,128)S(1)} %bitcast.136), channel_id=2, replica_groups=mesh['len'=128,'pipe'=4] {'len','pipe'}, dimensions={0}, use_global_device_ids=true | all-gather | bytes 525312 | tf_op jit(solution)/shard_map/all_gather | solution.py:139
  476.5 0.8 copy.58
  477.3 15.6 %all-to-all-start.3 = ((bf16[128,1,2,256]{3,2,1,0:T(2,128)(2,1)}), bf16[128,1,2,256]{3,2,1,0:T(2,128)(2,1)S(1)}, u32[]{:S(2)}, u32[]{:S(2)}) async-start(bf16[128,1,2,256]{3,2,1,0:T(2,128)(2,1)} %copy.58), calls=%async_computation.3 | async-start | bytes 262144 | tf_op jit(solution)/shard_map/all_to_all | solution.py:52
  493.0 12.8 %all-gather.1 = bf16[4,256,256]{2,1,0:T(8,128)(2,1)S(1)} all-gather(bf16[1,256,256]{2,1,0:T(8,128)(2,1)S(1)} %get-tuple-element.32), channel_id=3, replica_groups=mesh['len'=128,'pipe'=4] {'pipe'}, dimensions={0}, use_global_device_ids=true | all-gather | bytes 655360 | tf_op jit(solution)/shard_map/all_gather | solution.py:128
  505.8 0.8 convert_reduce_fusion.2
  506.5 13.4 %all-gather.2 = bf16[4,256,256]{2,1,0:T(8,128)(2,1)S(1)} all-gather(bf16[1,256,256]{2,1,0:T(8,128)(2,1)S(1)} %get-tuple-element.31), channel_id=4, replica_groups=mesh['len'=128,'pipe'=4] {'pipe'}, dimensions={0}, use_global_device_ids=true | all-gather | bytes 655360 | tf_op jit(solution)/shard_map/all_gather | solution.py:131
  519.9 0.8 convert_reduce_fusion.1
  521.3 1.8 copy.59
  523.2 1.3 scatter-add.6
  524.5 0.7 fusion.56
  525.2 1.3 scatter-add.9
  526.5 3.0 fusion.4
  (62 shorter events, 6.0 us)
Async XLA Ops:
  0.6 266.4 %copy-start = (bf16[256,256]{1,0:T(8,128)(2,1)S(1)}, bf16[256,256]{1,0:T(8,128)(2,1)}, u32[]{:S(2)}) copy-start(bf16[256,256]{1,0:T(8,128)(2,1)} %param.16) | copy-start | bytes 393220
  5.1 1.6 copy-start.3
  6.2 21.4 %copy-start.10 = (s32[512]{0:T(512)S(1)}, s32[512]{0:T(512)}, u32[]{:S(2)}) copy-start(s32[512]{0:T(512)} %param.22) | copy-start | bytes 6148
  6.2 22.0 %copy-start.11 = (s32[512]{0:T(512)S(1)}, s32[512]{0:T(512)}, u32[]{:S(2)}) copy-start(s32[512]{0:T(512)} %param.23) | copy-start | bytes 6148
  6.7 22.1 %copy-start.6 = (bf16[1,256,256]{2,1,0:T(8,128)(2,1)S(1)}, bf16[1,256,256]{2,1,0:T(8,128)(2,1)}, u32[]{:S(2)}) copy-start(bf16[1,256,256]{2,1,0:T(8,128)(2,1)} %param.19) | copy-start | bytes 393220
  7.8 223.9 %all-to-all-start = ((bf16[1,128,2,256]{3,2,0,1:T(2,128)(2,1)}), bf16[1,128,2,256]{3,2,0,1:T(2,128)(2,1)S(1)}, u32[]{:S(2)}, u32[]{:S(2)}) async-start(bf16[1,128,2,256]{3,2,0,1:T(2,128)(2,1)} %bitcast.6), calls=%async_computation | async-start | bytes 262144 | tf_op jit(solution)/shard_map/all_to_all | solution.py:48
  28.8 203.0 %copy-start.8 = (bf16[1,256,256]{2,1,0:T(8,128)(2,1)}, bf16[1,256,256]{2,1,0:T(8,128)(2,1)S(1)}, u32[]{:S(2)}) copy-start(bf16[1,256,256]{2,1,0:T(8,128)(2,1)S(1)} %neg.22) | copy-start | bytes 393220
  30.2 221.1 %copy-start.12 = (s32[2]{0:T(128)}, s32[2]{0:T(128)S(1)}, u32[]{:S(2)}) copy-start(s32[2]{0:T(128)S(1)} %pad_add_fusion) | copy-start | bytes 28
  34.6 197.2 %copy-start.15 = (bf16[1,256,256]{2,1,0:T(8,128)(2,1)S(1)}, bf16[1,256,256]{2,1,0:T(8,128)(2,1)}, u32[]{:S(2)}) copy-start(bf16[1,256,256]{2,1,0:T(8,128)(2,1)} %param.18) | copy-start | bytes 393220
  233.0 32.5 %all-to-all-start.1 = ((bf16[128,1,2,256]{3,2,1,0:T(2,128)(2,1)}), bf16[128,1,2,256]{3,2,1,0:T(2,128)(2,1)}, u32[]{:S(2)}, u32[]{:S(2)}) async-start(bf16[128,1,2,256]{3,2,1,0:T(2,128)(2,1)} %copy.50), calls=%async_computation.1 | async-start | bytes 262144 | tf_op jit(solution)/shard_map/all_to_all | solution.py:52
  251.4 15.7 %copy-start.4 = (bf16[1,2048,256]{2,1,0:T(8,128)(2,1)S(1)}, bf16[1,2048,256]{2,1,0:T(8,128)(2,1)}, u32[]{:S(2)}) copy-start(bf16[1,2048,256]{2,1,0:T(8,128)(2,1)} %param.14) | copy-start | bytes 3145732
  266.4 1.2 copy-start.14
  271.3 1.0 copy-start.1
  271.3 204.0 %copy-start.13 = (s32[2]{0:T(128)S(1)}, s32[2]{0:T(128)}, u32[]{:S(2)}) copy-start(s32[2]{0:T(128)} %copy-done.12) | copy-start | bytes 28
  271.4 204.3 %copy-start.5 = (bf16[256,256]{1,0:T(8,128)(2,1)S(1)}, bf16[256,256]{1,0:T(8,128)(2,1)}, u32[]{:S(2)}) copy-start(bf16[256,256]{1,0:T(8,128)(2,1)} %param.20) | copy-start | bytes 393220
  272.3 203.6 %copy-start.7 = (bf16[1,256,256]{2,1,0:T(8,128)(2,1)S(1)}, bf16[1,256,256]{2,1,0:T(8,128)(2,1)}, u32[]{:S(2)}) copy-start(bf16[1,256,256]{2,1,0:T(8,128)(2,1)} %param.19) | copy-start | bytes 393220
  272.3 203.6 %copy-start.9 = (bf16[1,256,256]{2,1,0:T(8,128)(2,1)S(1)}, bf16[1,256,256]{2,1,0:T(8,128)(2,1)}, u32[]{:S(2)}) copy-start(bf16[1,256,256]{2,1,0:T(8,128)(2,1)} %copy-done.8) | copy-start | bytes 393220
  272.3 203.6 %copy-start.16 = (bf16[1,256,256]{2,1,0:T(8,128)(2,1)S(1)}, bf16[1,256,256]{2,1,0:T(8,128)(2,1)}, u32[]{:S(2)}) copy-start(bf16[1,256,256]{2,1,0:T(8,128)(2,1)} %param.18) | copy-start | bytes 393220
  273.5 202.3 %all-to-all-start.2 = ((bf16[1,128,2,256]{3,2,0,1:T(2,128)(2,1)}), bf16[1,128,2,256]{3,2,0,1:T(2,128)(2,1)S(1)}, u32[]{:S(2)}, u32[]{:S(2)}) async-start(bf16[1,128,2,256]{3,2,0,1:T(2,128)(2,1)} %bitcast.19), calls=%async_computation.2 | async-start | bytes 262144 | tf_op jit(solution)/shard_map/all_to_all | solution.py:48
  477.3 43.4 %all-to-all-start.3 = ((bf16[128,1,2,256]{3,2,1,0:T(2,128)(2,1)}), bf16[128,1,2,256]{3,2,1,0:T(2,128)(2,1)S(1)}, u32[]{:S(2)}, u32[]{:S(2)}) async-start(bf16[128,1,2,256]{3,2,1,0:T(2,128)(2,1)} %copy.58), calls=%async_computation.3 | async-start | bytes 262144 | tf_op jit(solution)/shard_map/all_to_all | solution.py:52
  521.3 5.2 copy-start.2
where the time goes:
time: 530 us
  blocking collectives  416 us (78%)
  starting transfers between devices  58.9 us (11%)
  local copies, waits for them, and re-layouts  16.1 us (3%)
  other arithmetic  12.6 us (2%)
  waiting for transfers between devices  12.6 us (2%)
  matrix products  12.3 us (2%)
    all_gather x1, blocking collectives, body(): lax.all_gather(jnp.stack([inputs[:, 0, :], inputs[:, -1, :]]), ('len', 'p...  196 us
    all_gather x1, blocking collectives, body(): all_cond = lax.all_gather(grad_cond, ('len', 'pipe'), axis=0, tiled=True)  194 us
    all_to_all x2, starting transfers between devices, from_modes(): return lax.all_to_all(field, 'len', split_axis=0, concat_axis=1, tiled=True)  31.7 us
    all_to_all x2, starting transfers between devices, to_modes(): return lax.all_to_all(field, 'len', split_axis=1, concat_axis=0, tiled=True)  27.2 us
    all_gather x1, blocking collectives, body(): lax.all_gather(imag_terms.astype(jnp.bfloat16), 'pipe').astype(jnp.float32)  13.4 us
    all_gather x1, blocking collectives, body(): lax.all_gather(real_terms.astype(jnp.bfloat16), 'pipe').astype(jnp.float32)  12.8 us
    all_to_all x2, waiting for transfers between devices, from_modes(): return lax.all_to_all(field, 'len', split_axis=0, concat_axis=1, tiled=True)  12.6 us
  transfers between devices with their start and end apart: 4, of which 1 were waited for; matrix products, arithmetic and copies ran while one was open for 3% of the time, Pallas kernels for 0%

commit v1 on v0

--- a/solution.py
+++ b/solution.py
@@ -136,7 +136,8 @@
     )
     grad_cells = jnp.einsum("kl,pkc->plc", forward, grad_back, preferred_element_type=jnp.float32)
     grad_cond = jnp.sum(grad_total, axis=1, dtype=jnp.float32)
-    all_cond = lax.all_gather(grad_cond, ("len", "pipe"), axis=0, tiled=True)
+    sent = jnp.stack([grad_cond] * lax.axis_size(("len", "pipe")))
+    all_cond = jnp.concatenate(lax.all_to_all(sent, ("len", "pipe"), 0, 0), axis=0)
     junc_grad = COUPLING * jnp.dot(
         in_match.astype(jnp.float32) + out_match.astype(jnp.float32),
         all_cond,

time: 530 us -> 379 us (0.72)
  the two profiles are of different devices: /device:TPU:16 before, /device:TPU:1 now
where the time goes in v1:
time: 379 us; the launch traced here: 378 us
  blocking collectives  270 us (71%)
  starting transfers between devices  47.7 us (13%)
  waiting for transfers between devices  18.3 us (5%)
  local copies, waits for them, and re-layouts  15.8 us (4%)
  matrix products  13.3 us (4%)
  other arithmetic  12.6 us (3%)
    all_gather x1, blocking collectives, body(): lax.all_gather(jnp.stack([inputs[:, 0, :], inputs[:, -1, :]]), ('len', 'p...  197 us
    all_to_all x1, blocking collectives, to_modes(): return lax.all_to_all(field, 'len', split_axis=1, concat_axis=0, tiled=True)  23.8 us
    all_to_all x1, blocking collectives, from_modes(): return lax.all_to_all(field, 'len', split_axis=0, concat_axis=1, tiled=True)  23.8 us
    all_to_all x1, starting transfers between devices, to_modes(): return lax.all_to_all(field, 'len', split_axis=1, concat_axis=0, tiled=True)  20.6 us
    all_to_all x1, starting transfers between devices, from_modes(): return lax.all_to_all(field, 'len', split_axis=0, concat_axis=1, tiled=True)  14.4 us
    all_to_all x1, waiting for transfers between devices, from_modes(): return lax.all_to_all(field, 'len', split_axis=0, concat_axis=1, tiled=True)  13.1 us
    all_gather x1, blocking collectives, body(): lax.all_gather(real_terms.astype(jnp.bfloat16), 'pipe').astype(jnp.float32)  13 us
    all_to_all x1, starting transfers between devices, body(): lax.all_to_all(sent, ('len', 'pipe'), 0, 0)  12.7 us
  transfers between devices with their start and end apart: 3, of which 2 were waited for; matrix products, arithmetic and copies ran while one was open for 4% of the time, Pallas kernels for 0%

profile of v1, /device:TPU:1, one launch (start us, length us, event | category | flops | bytes accessed | tf_op | source)
XLA Modules:
  0.0 378.4 jit_solution(18236571204453687937)
XLA Ops:
  0.6 4.3 %negate_convert_fusion = (bf16[128,1,2048]{2,0,1:T(8,128)(2,1)S(1)}, bf16[128,1,2048]{2,0,1:T(8,128)(2,1)S(1)}) fusion(), kind=kLoop, calls=%fused_computation.57 | loop fusion | flops 4980736 | bytes 1048576 | tf_op jit(solution)/shard_map/convert.6
  5.1 1.1 copy.48
  7.1 0.7 reshape.324
  7.8 20.6 %all-to-all-start = ((bf16[1,128,2,256]{3,2,0,1:T(2,128)(2,1)}), bf16[1,128,2,256]{3,2,0,1:T(2,128)(2,1)S(1)}, u32[]{:S(2)}, u32[]{:S(2)}) async-start(bf16[1,128,2,256]{3,2,0,1:T(2,128)(2,1)} %bitcast.6), calls=%async_computation | async-start | bytes 262144 | tf_op jit(solution)/shard_map/all_to_all | solution.py:48
  29.7 1.4 pad_add_fusion
  31.1 4.4 %multiply_convert_fusion.1 = (bf16[128,1,2048]{2,0,1:T(8,128)(2,1)S(1)}, bf16[128,1,2048]{2,0,1:T(8,128)(2,1)S(1)}) fusion(f32[128]{0:T(128)S(1)} %negate_multiply_fusion, f32[128]{0:T(128)S(1)} %fusion.60), kind=kLoop, calls=%fused_computation.55 | loop fusion | flops 4718592 | bytes 1049600 | tf_op jit(solution)/shard_map/convert.4
  35.6 197.2 %all_gather.15 = bf16[2,512,256]{2,0,1:T(2,128)(2,1)S(1)} all-gather(bf16[2,1,256]{2,0,1:T(2,128)(2,1)S(1)} %pad_maximum_fusion.2), channel_id=1, replica_groups=mesh['len'=128,'pipe'=4] {'len','pipe'}, dimensions={1}, use_global_device_ids=true | all-gather | bytes 525312 | tf_op jit(solution)/shard_map/all_gather | solution.py:79
  232.8 1.5 fusion.64
  234.7 0.8 copy.50
  235.5 14.4 %all-to-all-start.1 = ((bf16[128,1,2,256]{3,2,1,0:T(2,128)(2,1)}), bf16[128,1,2,256]{3,2,1,0:T(2,128)(2,1)}, u32[]{:S(2)}, u32[]{:S(2)}) async-start(bf16[128,1,2,256]{3,2,1,0:T(2,128)(2,1)} %copy.50), calls=%async_computation.1 | async-start | bytes 262144 | tf_op jit(solution)/shard_map/all_to_all | solution.py:52
  249.9 0.8 fusion.39
  250.7 1.1 copy.51
  252.2 1.5 fusion.54
  253.8 13.1 %all-to-all-done.1 = bf16[128,1,2,256]{3,2,1,0:T(2,128)(2,1)} async-done(((bf16[128,1,2,256]{3,2,1,0:T(2,128)(2,1)}), bf16[128,1,2,256]{3,2,1,0:T(2,128)(2,1)}, u32[]{:S(2)}, u32[]{:S(2)}) %all-to-all-start.1) | async-done | bytes 131104 | tf_op jit(solution)/shard_map/all_to_all | solution.py:52
  266.8 1.0 reshape.327
  269.0 3.7 convert_reduce_fusion
  272.7 1.0 copy-done.1
  274.2 23.8 %all_to_all.20 = bf16[1,128,2,256]{3,2,0,1:T(2,128)(2,1)S(1)} all-to-all(bf16[1,128,2,256]{3,2,0,1:T(2,128)(2,1)S(1)} %bitcast.128), channel_id=1, replica_groups=mesh['len'=128,'pipe'=4] {'len'}, dimensions={1} | all-to-all | bytes 262144 | tf_op jit(solution)/shard_map/all_to_all | solution.py:48
  298.5 23.8 %all_to_all.42 = bf16[128,1,2,256]{3,2,1,0:T(2,128)(2,1)S(1)} all-to-all(bf16[128,1,2,256]{3,2,1,0:T(2,128)(2,1)S(1)} %copy.58), channel_id=1, replica_groups=mesh['len'=128,'pipe'=4] {'len'}, dimensions={0} | all-to-all | bytes 262144 | tf_op jit(solution)/shard_map/all_to_all | solution.py:52
  322.3 1.1 stack.13
  323.4 12.7 %all-to-all-start.4 = ((f32[512,1,256]{2,1,0:T(1,128)}), f32[512,1,256]{2,1,0:T(1,128)}, u32[]{:S(2)}, u32[]{:S(2)}) async-start(f32[512,1,256]{2,1,0:T(1,128)} %stack.13), calls=%async_computation.4 | async-start | bytes 1048576 | tf_op jit(solution)/shard_map/all_to_all | solution.py:140
  336.5 13.0 %all-gather = bf16[4,256,256]{2,1,0:T(8,128)(2,1)S(1)} all-gather(bf16[1,256,256]{2,1,0:T(8,128)(2,1)S(1)} %get-tuple-element.32), channel_id=2, replica_groups=mesh['len'=128,'pipe'=4] {'pipe'}, dimensions={0}, use_global_device_ids=true | all-gather | bytes 655360 | tf_op jit(solution)/shard_map/all_gather | solution.py:128
  349.5 0.8 convert_reduce_fusion.2
  350.3 11.6 %all-gather.1 = bf16[4,256,256]{2,1,0:T(8,128)(2,1)S(1)} all-gather(bf16[1,256,256]{2,1,0:T(8,128)(2,1)S(1)} %get-tuple-element.31), channel_id=3, replica_groups=mesh['len'=128,'pipe'=4] {'pipe'}, dimensions={0}, use_global_device_ids=true | all-gather | bytes 655360 | tf_op jit(solution)/shard_map/all_gather | solution.py:131
  361.9 0.8 convert_reduce_fusion.1
  363.2 1.8 copy.59
  365.2 5.2 %all-to-all-done.4 = f32[512,1,256]{2,1,0:T(1,128)} async-done(((f32[512,1,256]{2,1,0:T(1,128)}), f32[512,1,256]{2,1,0:T(1,128)}, u32[]{:S(2)}, u32[]{:S(2)}) %all-to-all-start.4) | async-done | bytes 524320 | tf_op jit(solution)/shard_map/all_to_all | solution.py:140
  370.4 1.4 fusion.22
  372.0 1.3 scatter-add.6
  373.3 0.7 fusion.56
  374.0 1.3 scatter-add.9
  375.3 3.0 fusion.4
  (62 shorter events, 6.5 us)
Async XLA Ops:
  0.6 267.8 %copy-start = (bf16[256,256]{1,0:T(8,128)(2,1)S(1)}, bf16[256,256]{1,0:T(8,128)(2,1)}, u32[]{:S(2)}) copy-start(bf16[256,256]{1,0:T(8,128)(2,1)} %param.16) | copy-start | bytes 393220
  5.1 1.6 copy-start.3
  6.2 22.3 %copy-start.10 = (s32[512]{0:T(512)S(1)}, s32[512]{0:T(512)}, u32[]{:S(2)}) copy-start(s32[512]{0:T(512)} %param.22) | copy-start | bytes 6148
  6.2 22.9 %copy-start.11 = (s32[512]{0:T(512)S(1)}, s32[512]{0:T(512)}, u32[]{:S(2)}) copy-start(s32[512]{0:T(512)} %param.23) | copy-start | bytes 6148
  6.7 23.0 %copy-start.5 = (bf16[1,256,256]{2,1,0:T(8,128)(2,1)S(1)}, bf16[1,256,256]{2,1,0:T(8,128)(2,1)}, u32[]{:S(2)}) copy-start(bf16[1,256,256]{2,1,0:T(8,128)(2,1)} %param.19) | copy-start | bytes 393220
  7.8 226.5 %all-to-all-start = ((bf16[1,128,2,256]{3,2,0,1:T(2,128)(2,1)}), bf16[1,128,2,256]{3,2,0,1:T(2,128)(2,1)S(1)}, u32[]{:S(2)}, u32[]{:S(2)}) async-start(bf16[1,128,2,256]{3,2,0,1:T(2,128)(2,1)} %bitcast.6), calls=%async_computation | async-start | bytes 262144 | tf_op jit(solution)/shard_map/all_to_all | solution.py:48
  29.7 204.7 %copy-start.8 = (bf16[1,256,256]{2,1,0:T(8,128)(2,1)}, bf16[1,256,256]{2,1,0:T(8,128)(2,1)S(1)}, u32[]{:S(2)}) copy-start(bf16[1,256,256]{2,1,0:T(8,128)(2,1)S(1)} %neg.22) | copy-start | bytes 393220
  31.1 221.1 %copy-start.12 = (s32[2]{0:T(128)}, s32[2]{0:T(128)S(1)}, u32[]{:S(2)}) copy-start(s32[2]{0:T(128)S(1)} %pad_add_fusion) | copy-start | bytes 28
  35.5 198.9 %copy-start.15 = (bf16[1,256,256]{2,1,0:T(8,128)(2,1)S(1)}, bf16[1,256,256]{2,1,0:T(8,128)(2,1)}, u32[]{:S(2)}) copy-start(bf16[1,256,256]{2,1,0:T(8,128)(2,1)} %param.18) | copy-start | bytes 393220
  235.5 31.3 %all-to-all-start.1 = ((bf16[128,1,2,256]{3,2,1,0:T(2,128)(2,1)}), bf16[128,1,2,256]{3,2,1,0:T(2,128)(2,1)}, u32[]{:S(2)}, u32[]{:S(2)}) async-start(bf16[128,1,2,256]{3,2,1,0:T(2,128)(2,1)} %copy.50), calls=%async_computation.1 | async-start | bytes 262144 | tf_op jit(solution)/shard_map/all_to_all | solution.py:52
  252.2 16.2 %copy-start.4 = (bf16[1,2048,256]{2,1,0:T(8,128)(2,1)S(1)}, bf16[1,2048,256]{2,1,0:T(8,128)(2,1)}, u32[]{:S(2)}) copy-start(bf16[1,2048,256]{2,1,0:T(8,128)(2,1)} %param.14) | copy-start | bytes 3145732
  267.8 1.2 copy-start.14
  272.7 1.0 copy-start.1
  272.7 25.3 %copy-start.6 = (bf16[1,256,256]{2,1,0:T(8,128)(2,1)S(1)}, bf16[1,256,256]{2,1,0:T(8,128)(2,1)}, u32[]{:S(2)}) copy-start(bf16[1,256,256]{2,1,0:T(8,128)(2,1)} %param.19) | copy-start | bytes 393220
  272.7 25.3 %copy-start.9 = (bf16[1,256,256]{2,1,0:T(8,128)(2,1)S(1)}, bf16[1,256,256]{2,1,0:T(8,128)(2,1)}, u32[]{:S(2)}) copy-start(bf16[1,256,256]{2,1,0:T(8,128)(2,1)} %copy-done.8) | copy-start | bytes 393220
  272.7 25.4 %copy-start.16 = (bf16[1,256,256]{2,1,0:T(8,128)(2,1)S(1)}, bf16[1,256,256]{2,1,0:T(8,128)(2,1)}, u32[]{:S(2)}) copy-start(bf16[1,256,256]{2,1,0:T(8,128)(2,1)} %param.18) | copy-start | bytes 393220
  323.4 47.0 %all-to-all-start.4 = ((f32[512,1,256]{2,1,0:T(1,128)}), f32[512,1,256]{2,1,0:T(1,128)}, u32[]{:S(2)}, u32[]{:S(2)}) async-start(f32[512,1,256]{2,1,0:T(1,128)} %stack.13), calls=%async_computation.4 | async-start | bytes 1048576 | tf_op jit(solution)/shard_map/all_to_all | solution.py:140
  363.2 7.2 %copy-start.13 = (s32[2]{0:T(128)S(1)}, s32[2]{0:T(128)}, u32[]{:S(2)}) copy-start(s32[2]{0:T(128)} %copy-done.12) | copy-start | bytes 28
  363.2 8.6 %copy-start.7 = (bf16[256,256]{1,0:T(8,128)(2,1)S(1)}, bf16[256,256]{1,0:T(8,128)(2,1)}, u32[]{:S(2)}) copy-start(bf16[256,256]{1,0:T(8,128)(2,1)} %param.20) | copy-start | bytes 393220
  363.2 12.1 %copy-start.2 = (bf16[1,2048,256]{2,1,0:T(8,128)(2,1)S(1)}, bf16[1,2048,256]{2,1,0:T(8,128)(2,1)}, u32[]{:S(2)}) copy-start(bf16[1,2048,256]{2,1,0:T(8,128)(2,1)} %copy-done.1) | copy-start | bytes 3145732
